TPU v7x, 32 devices: a whole 2x2x4 slice. The times are simulated.
32 devices in a mesh: groups: 2 (over y), seq: 8 (over z, x), enc: 2 (over core).
Axes of the slice: x: 2, y: 2, z: 4, core: 2. Of those that a mesh axis runs over, the one named last changes fastest.
Arguments:
- self_queries: bfloat16 [2, 256, 4096], P('enc', ('groups', 'seq')), parts along dimension 1, may hold values from -32 to 32
- self_keys: bfloat16 [2, 256, 4096], P('enc', ('groups', 'seq')), parts along dimension 1, may hold values from -32 to 32
- self_values: bfloat16 [2, 256, 4096], P('enc', ('groups', 'seq')), parts along dimension 1, may hold values from -6 to 6
- text_queries: bfloat16 [2, 256, 4096], P('enc', ('groups', 'seq')), parts along dimension 1, may hold values from -32 to 32
- text_kv: bfloat16 [2, 2, 1024, 4096], P('enc', None, ('groups', 'seq')), parts along dimension 2, may hold values from -32 to 32
- text_len: int32 [4], P('groups'), parts along dimension 0, may hold values from 16 to 512
Outputs:
- self_mixed: bfloat16 [2, 256, 4096], P('enc', ('groups', 'seq')), parts along dimension 1
- text_mixed: bfloat16 [2, 256, 4096], P('enc', ('groups', 'seq')), parts along dimension 1
There are 2 independent parts, one for each index of `groups`. A program takes and returns all parts, laid end to end along the dimension named above; each array names one. Nothing has to cross between parts.
Inputs may be any that keep to these rules, and one draw needn't show every extreme that they name: `text_len`: entry 0 is the prompt's length, entry 1 the negative prompt's; text rows at or past a length are padding.
All inputs are finite; a program needn't handle non-finite values.
Results may differ from a plain program's by a relative error of at most 0.0034.
Values may be sent and summed in bfloat16 or wider, within the bound.
A program may use at most 64 MiB of HBM per device.

v0:
```python
import math

import jax
import jax.numpy as jnp
from jax import lax
from jax.sharding import PartitionSpec as P

HEADS = 32
HEAD_DIM = 128


def absorb(run_state, queries, key_rows, value_rows, live_mask):
    running_max, row_total, weighted_sum = run_state
    scores = jnp.einsum(
        "qpd,kpd->pqk", queries, key_rows, preferred_element_type=jnp.float32
    ) / math.sqrt(HEAD_DIM)
    scores = jnp.where(live_mask[None, None, :], scores, -1e30)
    new_max = jnp.maximum(running_max, jnp.max(scores, axis=2))
    weights = jnp.where(live_mask[None, None, :], jnp.exp(scores - new_max[:, :, None]), 0.0)
    factor = jnp.exp(running_max - new_max)
    row_total = row_total * factor + jnp.sum(weights, axis=2)
    weighted_sum = weighted_sum * factor[:, :, None] + jnp.einsum(
        "pqk,kpd->pqd", weights.astype(jnp.bfloat16), value_rows, preferred_element_type=jnp.float32
    )
    return (new_max, row_total, weighted_sum)


def empty_state(head_count, query_count):
    return (
        jnp.full((head_count, query_count), -1e30, jnp.float32),
        jnp.zeros((head_count, query_count), jnp.float32),
        jnp.zeros((head_count, query_count, HEAD_DIM), jnp.float32),
    )


def finish(run_state):
    running_max, row_total, weighted_sum = run_state
    return (weighted_sum / row_total[:, :, None]).transpose(1, 0, 2).astype(jnp.bfloat16)


def block_attention(queries, key_rows, value_rows, live_mask):
    query_total, heads_here, head_width = queries.shape
    key_total = key_rows.shape[0]
    key_block = 1024 if key_total % 1024 == 0 else key_total
    query_block = 512 if query_total % 512 == 0 else query_total
    key_blocks = key_rows.reshape(key_total // key_block, key_block, heads_here, head_width)
    value_blocks = value_rows.reshape(key_total // key_block, key_block, heads_here, head_width)
    live_blocks = live_mask.reshape(key_total // key_block, key_block)

    def one_block(query_piece):

        def absorb_block(run_state, pieces):
            return (absorb(run_state, query_piece, pieces[0], pieces[1], pieces[2]), None)

        final_state, unused = lax.scan(
            absorb_block,
            empty_state(heads_here, query_block),
            (key_blocks, value_blocks, live_blocks),
        )
        return finish(final_state)

    blended = lax.map(
        one_block, queries.reshape(query_total // query_block, query_block, heads_here, head_width)
    )
    return blended.reshape(query_total, heads_here, head_width)


def shards(self_queries, self_keys, self_values, text_queries, text_kv, text_len):
    token_rows = self_queries.shape[1]
    channel_count = self_queries.shape[2]
    seq_count = lax.axis_size("seq")
    quarter_count = max(seq_count // HEADS, 1)
    heads_here = max(HEADS // seq_count, 1)
    group_count = HEADS // heads_here
    head_span = heads_here * HEAD_DIM
    share_rows = token_rows // quarter_count
    query_total = share_rows * seq_count
    branch = lax.axis_index("enc")
    length = lax.dynamic_index_in_dim(text_len, branch, 0, keepdims=False)

    def head_view(tensor):
        return tensor.reshape(1, share_rows, seq_count, head_span)

    def repeated(tensor):
        spread = jnp.broadcast_to(
            tensor.reshape(1, token_rows, 1, group_count, head_span),
            (1, token_rows, quarter_count, group_count, head_span),
        )
        return spread.reshape(1, token_rows, seq_count, head_span)

    head_queries, head_keys, head_values = (
        lax.all_to_all(head_view(self_queries), "seq", split_axis=2, concat_axis=1, tiled=True),
        lax.all_to_all(repeated(self_keys), "seq", split_axis=2, concat_axis=1, tiled=True),
        lax.all_to_all(repeated(self_values), "seq", split_axis=2, concat_axis=1, tiled=True),
    )
    key_rows = head_keys.reshape(-1, heads_here, HEAD_DIM)
    value_rows = head_values.reshape(-1, heads_here, HEAD_DIM)
    query_rows = head_queries.reshape(query_total, heads_here, HEAD_DIM)
    every_key = jnp.ones((key_rows.shape[0],), jnp.bool_)
    self_heads = block_attention(query_rows, key_rows, value_rows, every_key)
    head_text_queries = lax.all_to_all(
        head_view(text_queries), "seq", split_axis=2, concat_axis=1, tiled=True
    )
    context_rows = text_kv.shape[2]
    spread = jnp.broadcast_to(
        text_kv.reshape(1, 2, context_rows, 1, group_count, head_span),
        (1, 2, context_rows, quarter_count, group_count, head_span),
    )
    head_context = lax.all_to_all(
        spread.reshape(1, 2, context_rows, seq_count, head_span),
        "seq",
        split_axis=3,
        concat_axis=2,
        tiled=True,
    )
    text_total = head_context.shape[2]
    context_keys = head_context[0, 0].reshape(text_total, heads_here, HEAD_DIM)
    context_values = head_context[0, 1].reshape(text_total, heads_here, HEAD_DIM)
    live_mask = jnp.arange(text_total, dtype=jnp.int32) < length
    text_heads = block_attention(
        head_text_queries.reshape(query_total, heads_here, HEAD_DIM),
        context_keys,
        context_values,
        live_mask,
    )
    self_view = self_heads.reshape(1, seq_count, share_rows, 1, head_span)
    text_view = text_heads.reshape(1, seq_count, share_rows, 1, head_span)
    self_back, text_back = (
        lax.all_to_all(self_view, "seq", split_axis=1, concat_axis=3, tiled=True),
        lax.all_to_all(text_view, "seq", split_axis=1, concat_axis=3, tiled=True),
    )
    self_mixed = self_back.reshape(1, token_rows, channel_count)
    text_mixed = text_back.reshape(1, token_rows, channel_count)
    return (self_mixed, text_mixed)


def solution(mesh):
    return jax.shard_map(
        shards,
        mesh=mesh,
        in_specs=(
            P("enc", ("groups", "seq"), None),
            P("enc", ("groups", "seq"), None),
            P("enc", ("groups", "seq"), None),
            P("enc", ("groups", "seq"), None),
            P("enc", None, ("groups", "seq"), None),
            P("groups"),
        ),
        out_specs=(P("enc", ("groups", "seq"), None), P("enc", ("groups", "seq"), None)),
        check_vma=False,
    )
```

profile of v0, /device:TPU:0, one launch (start us, length us, event | category | flops | bytes accessed | tf_op | source)
XLA Modules:
  0.0 96.1 jit_solution(9407266434773647856)
XLA Ops:
  0.6 0.0 copy-start
  0.6 1.7 %copy.108 = bf16[1,2,8,8,512]{4,3,1,0,2:T(8,128)(2,1)} copy(bf16[1,2,8,8,512]{4,3,2,1,0:T(8,128)(2,1)} %bitcast.112) | data formatting | bytes 262144 | tf_op jit(solution)/shard_map/reshape | solution.py:82
  2.3 7.3 %all-to-all-start.4 = ((bf16[1,16,8,512]{3,1,0,2:T(8,128)(2,1)}), bf16[1,16,8,512]{3,1,0,2:T(8,128)(2,1)S(1)}, u32[]{:S(2)}, u32[]{:S(2)}) async-start(bf16[1,16,8,512]{3,1,0,2:T(8,128)(2,1)} %bitcast.98), calls=%async_computation.4 | async-start | bytes 262144 | tf_op jit(solution)/shard_map/all_to_all | solution.py:101
  9.6 1.6 %copy.111 = bf16[1,2,8,8,512]{4,3,1,0,2:T(8,128)(2,1)} copy(bf16[1,2,8,8,512]{4,3,2,1,0:T(8,128)(2,1)} %bitcast.113) | data formatting | bytes 262144 | tf_op jit(solution)/shard_map/reshape | solution.py:82
  11.1 5.8 %all-to-all-done.4 = bf16[1,16,8,512]{3,1,0,2:T(8,128)(2,1)S(1)} async-done(((bf16[1,16,8,512]{3,1,0,2:T(8,128)(2,1)}), bf16[1,16,8,512]{3,1,0,2:T(8,128)(2,1)S(1)}, u32[]{:S(2)}, u32[]{:S(2)}) %all-to-all-start.4) | async-done | bytes 131104 | tf_op jit(solution)/shard_map/all_to_all | solution.py:101
  16.9 3.4 %all-to-all-start = ((bf16[1,16,8,512]{3,1,0,2:T(8,128)(2,1)}), bf16[1,16,8,512]{3,1,0,2:T(8,128)(2,1)S(1)}, u32[]{:S(2)}, u32[]{:S(2)}) async-start(bf16[1,16,8,512]{3,1,0,2:T(8,128)(2,1)} %bitcast.101), calls=%async_computation | async-start | bytes 262144 | tf_op jit(solution)/shard_map/all_to_all | solution.py:92
  20.3 1.6 %copy.110 = bf16[1,2,8,8,512]{4,3,1,0,2:T(8,128)(2,1)} copy(bf16[1,2,8,8,512]{4,3,2,1,0:T(8,128)(2,1)} %bitcast.114) | data formatting | bytes 262144 | tf_op jit(solution)/shard_map/reshape;reshape | solution.py:89
  21.9 5.7 %all-to-all-done = bf16[1,16,8,512]{3,1,0,2:T(8,128)(2,1)S(1)} async-done(((bf16[1,16,8,512]{3,1,0,2:T(8,128)(2,1)}), bf16[1,16,8,512]{3,1,0,2:T(8,128)(2,1)S(1)}, u32[]{:S(2)}, u32[]{:S(2)}) %all-to-all-start) | async-done | bytes 131104 | tf_op jit(solution)/shard_map/all_to_all | solution.py:92
  27.6 0.0 copy-start.1
  27.6 3.5 %all-to-all-start.1 = ((bf16[1,16,8,512]{3,1,0,2:T(8,128)(2,1)}), bf16[1,16,8,512]{3,1,0,2:T(8,128)(2,1)S(1)}, u32[]{:S(2)}, u32[]{:S(2)}) async-start(bf16[1,16,8,512]{3,1,0,2:T(8,128)(2,1)} %bitcast.100), calls=%async_computation.1 | async-start | bytes 262144 | tf_op jit(solution)/shard_map/all_to_all | solution.py:93
  31.1 0.0 copy-done.1
  31.1 0.7 copy.109
  31.8 6.6 %all-to-all-done.1 = bf16[1,16,8,512]{3,1,0,2:T(8,128)(2,1)S(1)} async-done(((bf16[1,16,8,512]{3,1,0,2:T(8,128)(2,1)}), bf16[1,16,8,512]{3,1,0,2:T(8,128)(2,1)S(1)}, u32[]{:S(2)}, u32[]{:S(2)}) %all-to-all-start.1) | async-done | bytes 131104 | tf_op jit(solution)/shard_map/all_to_all | solution.py:93
  38.4 3.4 %all-to-all-start.2 = ((bf16[1,16,8,512]{3,1,0,2:T(8,128)(2,1)}), bf16[1,16,8,512]{3,1,0,2:T(8,128)(2,1)S(1)}, u32[]{:S(2)}, u32[]{:S(2)}) async-start(bf16[1,16,8,512]{3,1,0,2:T(8,128)(2,1)} %bitcast.99), calls=%async_computation.2 | async-start | bytes 262144 | tf_op jit(solution)/shard_map/all_to_all | solution.py:94
  41.8 0.0 copy-done
  41.8 1.1 %copy.107 = bf16[1,2,8,8,8,512]{5,4,2,1,0,3:T(8,128)(2,1)} copy(bf16[1,2,8,8,8,512]{5,4,3,2,1,0:T(8,128)(2,1)S(1)} %bitcast.104) | data formatting | bytes 2097152 | tf_op jit(solution)/shard_map/reshape;reshape | solution.py:110
  42.9 6.2 %all-to-all-done.2 = bf16[1,16,8,512]{3,1,0,2:T(8,128)(2,1)S(1)} async-done(((bf16[1,16,8,512]{3,1,0,2:T(8,128)(2,1)}), bf16[1,16,8,512]{3,1,0,2:T(8,128)(2,1)S(1)}, u32[]{:S(2)}, u32[]{:S(2)}) %all-to-all-start.2) | async-done | bytes 131104 | tf_op jit(solution)/shard_map/all_to_all | solution.py:94
  49.0 3.6 %all-to-all-start.5 = ((bf16[1,2,64,8,512]{4,2,1,0,3:T(8,128)(2,1)}), bf16[1,2,64,8,512]{4,2,1,0,3:T(8,128)(2,1)S(1)}, u32[]{:S(2)}, u32[]{:S(2)}) async-start(bf16[1,2,64,8,512]{4,2,1,0,3:T(8,128)(2,1)} %bitcast.97), calls=%async_computation.5 | async-start | bytes 2097152 | tf_op jit(solution)/shard_map/all_to_all | solution.py:109
  52.6 0.0 copy-start.2
  52.6 0.6 copy-done.2
  53.3 0.6 dynamic_slice.30
  53.9 0.6 iota_compare_fusion
  54.7 0.2 fusion.23
  54.9 0.1 fusion.13
  55.0 0.3 fusion.5
  55.3 0.1 copy.66
  55.4 0.7 reshape_reshape.21
  56.1 17.8 %all-to-all-done.5 = bf16[1,2,64,8,512]{4,2,1,0,3:T(8,128)(2,1)S(1)} async-done(((bf16[1,2,64,8,512]{4,2,1,0,3:T(8,128)(2,1)}), bf16[1,2,64,8,512]{4,2,1,0,3:T(8,128)(2,1)S(1)}, u32[]{:S(2)}, u32[]{:S(2)}) %all-to-all-start.5) | async-done | bytes 1048608 | tf_op jit(solution)/shard_map/all_to_all | solution.py:109
  73.9 3.4 %all-to-all-start.3 = ((bf16[1,8,16,1,512]{4,2,3,0,1:T(8,128)(2,1)}), bf16[1,8,16,1,512]{4,2,3,0,1:T(8,128)(2,1)S(1)}, u32[]{:S(2)}, u32[]{:S(2)}) async-start(bf16[1,8,16,1,512]{4,2,3,0,1:T(8,128)(2,1)} %bitcast.9), calls=%async_computation.3 | async-start | bytes 262144 | tf_op jit(solution)/shard_map/all_to_all | solution.py:129
  77.3 0.1 copy.71
  77.4 0.1 fusion.22
  77.5 0.2 copy.72
  77.7 0.4 fusion.24
  78.1 0.3 fusion.7
  78.4 0.2 copy.75
  78.7 0.4 fusion.6
  79.0 0.1 copy.77
  79.1 0.7 reshape_reshape.23
  79.8 4.8 %all-to-all-done.3 = bf16[1,8,16,1,512]{4,2,3,0,1:T(8,128)(2,1)S(1)} async-done(((bf16[1,8,16,1,512]{4,2,3,0,1:T(8,128)(2,1)}), bf16[1,8,16,1,512]{4,2,3,0,1:T(8,128)(2,1)S(1)}, u32[]{:S(2)}, u32[]{:S(2)}) %all-to-all-start.3) | async-done | bytes 131104 | tf_op jit(solution)/shard_map/all_to_all | solution.py:129
  84.7 3.4 %all-to-all-start.6 = ((bf16[1,8,16,1,512]{4,2,3,0,1:T(8,128)(2,1)}), bf16[1,8,16,1,512]{4,2,3,0,1:T(8,128)(2,1)S(1)}, u32[]{:S(2)}, u32[]{:S(2)}) async-start(bf16[1,8,16,1,512]{4,2,3,0,1:T(8,128)(2,1)} %bitcast.25), calls=%async_computation.6 | async-start | bytes 262144 | tf_op jit(solution)/shard_map/all_to_all | solution.py:130
  88.0 0.1 copy.68
  88.1 0.7 reshape.65
  88.8 6.5 %all-to-all-done.6 = bf16[1,8,16,1,512]{4,2,3,0,1:T(8,128)(2,1)S(1)} async-done(((bf16[1,8,16,1,512]{4,2,3,0,1:T(8,128)(2,1)}), bf16[1,8,16,1,512]{4,2,3,0,1:T(8,128)(2,1)S(1)}, u32[]{:S(2)}, u32[]{:S(2)}) %all-to-all-start.6) | async-done | bytes 131104 | tf_op jit(solution)/shard_map/all_to_all | solution.py:130
  95.3 0.1 copy.79
  95.4 0.7 reshape.67
  (8 shorter events, 0.2 us)
Async XLA Ops:
  0.6 41.1 %copy-start = (bf16[1,2,64,4096]{3,2,1,0:T(8,128)(2,1)S(1)}, bf16[1,2,64,4096]{3,2,1,0:T(8,128)(2,1)}, u32[]{:S(2)}) copy-start(bf16[1,2,64,4096]{3,2,1,0:T(8,128)(2,1)} %param.10) | copy-start | bytes 3145732
  2.3 14.6 %all-to-all-start.4 = ((bf16[1,16,8,512]{3,1,0,2:T(8,128)(2,1)}), bf16[1,16,8,512]{3,1,0,2:T(8,128)(2,1)S(1)}, u32[]{:S(2)}, u32[]{:S(2)}) async-start(bf16[1,16,8,512]{3,1,0,2:T(8,128)(2,1)} %bitcast.98), calls=%async_computation.4 | async-start | bytes 262144 | tf_op jit(solution)/shard_map/all_to_all | solution.py:101
  16.9 10.7 %all-to-all-start = ((bf16[1,16,8,512]{3,1,0,2:T(8,128)(2,1)}), bf16[1,16,8,512]{3,1,0,2:T(8,128)(2,1)S(1)}, u32[]{:S(2)}, u32[]{:S(2)}) async-start(bf16[1,16,8,512]{3,1,0,2:T(8,128)(2,1)} %bitcast.101), calls=%async_computation | async-start | bytes 262144 | tf_op jit(solution)/shard_map/all_to_all | solution.py:92
  27.6 3.5 %copy-start.1 = (bf16[1,16,4096]{2,1,0:T(8,128)(2,1)S(1)}, bf16[1,16,4096]{2,1,0:T(8,128)(2,1)}, u32[]{:S(2)}) copy-start(bf16[1,16,4096]{2,1,0:T(8,128)(2,1)} %param.8) | copy-start | bytes 393220
  27.6 10.8 %all-to-all-start.1 = ((bf16[1,16,8,512]{3,1,0,2:T(8,128)(2,1)}), bf16[1,16,8,512]{3,1,0,2:T(8,128)(2,1)S(1)}, u32[]{:S(2)}, u32[]{:S(2)}) async-start(bf16[1,16,8,512]{3,1,0,2:T(8,128)(2,1)} %bitcast.100), calls=%async_computation.1 | async-start | bytes 262144 | tf_op jit(solution)/shard_map/all_to_all | solution.py:93
  38.4 10.7 %all-to-all-start.2 = ((bf16[1,16,8,512]{3,1,0,2:T(8,128)(2,1)}), bf16[1,16,8,512]{3,1,0,2:T(8,128)(2,1)S(1)}, u32[]{:S(2)}, u32[]{:S(2)}) async-start(bf16[1,16,8,512]{3,1,0,2:T(8,128)(2,1)} %bitcast.99), calls=%async_computation.2 | async-start | bytes 262144 | tf_op jit(solution)/shard_map/all_to_all | solution.py:94
  49.0 24.9 %all-to-all-start.5 = ((bf16[1,2,64,8,512]{4,2,1,0,3:T(8,128)(2,1)}), bf16[1,2,64,8,512]{4,2,1,0,3:T(8,128)(2,1)S(1)}, u32[]{:S(2)}, u32[]{:S(2)}) async-start(bf16[1,2,64,8,512]{4,2,1,0,3:T(8,128)(2,1)} %bitcast.97), calls=%async_computation.5 | async-start | bytes 2097152 | tf_op jit(solution)/shard_map/all_to_all | solution.py:109
  52.6 0.7 copy-start.2
  73.9 10.7 %all-to-all-start.3 = ((bf16[1,8,16,1,512]{4,2,3,0,1:T(8,128)(2,1)}), bf16[1,8,16,1,512]{4,2,3,0,1:T(8,128)(2,1)S(1)}, u32[]{:S(2)}, u32[]{:S(2)}) async-start(bf16[1,8,16,1,512]{4,2,3,0,1:T(8,128)(2,1)} %bitcast.9), calls=%async_computation.3 | async-start | bytes 262144 | tf_op jit(solution)/shard_map/all_to_all | solution.py:129
  84.7 10.7 %all-to-all-start.6 = ((bf16[1,8,16,1,512]{4,2,3,0,1:T(8,128)(2,1)}), bf16[1,8,16,1,512]{4,2,3,0,1:T(8,128)(2,1)S(1)}, u32[]{:S(2)}, u32[]{:S(2)}) async-start(bf16[1,8,16,1,512]{4,2,3,0,1:T(8,128)(2,1)} %bitcast.25), calls=%async_computation.6 | async-start | bytes 262144 | tf_op jit(solution)/shard_map/all_to_all | solution.py:130
where the time goes:
time: 97.1 us; the launch traced here: 96.1 us
  waiting for transfers between devices  53.4 us (55%)
  starting transfers between devices  27.9 us (29%)
  local copies, waits for them, and re-layouts  11.7 us (12%)
  matrix products  1.23 us (1%)
  other arithmetic  1.08 us (1%)
    all_to_all x1, waiting for transfers between devices, shards(): lax.all_to_all(spread.reshape(1, 2, context_rows, seq_count, head_span),...  17.8 us
    all_to_all x1, starting transfers between devices, shards(): lax.all_to_all(head_view(text_queries), 'seq', split_axis=2, concat_axis=...  7.28 us
    all_to_all x1, waiting for transfers between devices, shards(): lax.all_to_all(repeated(self_keys), 'seq', split_axis=2, concat_axis=1, t...  6.61 us
    all_to_all x1, waiting for transfers between devices, shards(): lax.all_to_all(text_view, 'seq', split_axis=1, concat_axis=3, tiled=True)  6.47 us
    all_to_all x1, waiting for transfers between devices, shards(): lax.all_to_all(repeated(self_values), 'seq', split_axis=2, concat_axis=1,...  6.18 us
    all_to_all x1, waiting for transfers between devices, shards(): lax.all_to_all(head_view(text_queries), 'seq', split_axis=2, concat_axis=...  5.78 us
    all_to_all x1, waiting for transfers between devices, shards(): lax.all_to_all(head_view(self_queries), 'seq', split_axis=2, concat_axis=...  5.71 us
    all_to_all x1, waiting for transfers between devices, shards(): lax.all_to_all(self_view, 'seq', split_axis=1, concat_axis=3, tiled=True)  4.83 us
  transfers between devices with their start and end apart: 7, of which 7 were waited for; matrix products, arithmetic and copies ran while one was open for 11% of the time, Pallas kernels for 0%

commit v1 on v0

--- a/solution.py
+++ b/solution.py
@@ -1,8 +1,11 @@
+import functools
 import math
 
 import jax
 import jax.numpy as jnp
 from jax import lax
+from jax.experimental import pallas as pl
+from jax.experimental.pallas import tpu as pltpu
 from jax.sharding import PartitionSpec as P
 
 HEADS = 32
@@ -134,9 +137,233 @@
     return (self_mixed, text_mixed)
 
 
+HALVES = 2
+MESH = pl.DeviceIdType.MESH
+FAR = -1e30
+
+
+def attend(queries, key_rows, value_rows, live):
+    scores = lax.dot_general(
+        queries, key_rows, (((1,), (1,)), ((), ())), preferred_element_type=jnp.float32
+    ) * (1.0 / math.sqrt(HEAD_DIM))
+    if live is not None:
+        scores = jnp.where(live, scores, FAR)
+    top = jnp.max(scores, axis=1, keepdims=True)
+    weights = jnp.exp(scores - top)
+    if live is not None:
+        weights = jnp.where(live, weights, 0.0)
+    total = jnp.sum(weights, axis=1, keepdims=True)
+    mixed = jnp.dot(weights.astype(jnp.bfloat16), value_rows, preferred_element_type=jnp.float32)
+    return mixed, top, total
+
+
+def fused(
+    count,
+    self_q,
+    self_k,
+    self_v,
+    text_q,
+    text_kv,
+    text_len,
+    self_out,
+    text_out,
+    own_q,
+    own_k,
+    own_v,
+    text_rows,
+    context,
+    self_part,
+    text_part,
+    stat_part,
+    text_back,
+    stat_back,
+    send_sem,
+    recv_sem,
+    local_sem,
+):
+    me = lax.axis_index("seq")
+    branch = lax.axis_index("enc")
+    ring = count // HALVES
+    half, place = lax.div(me, ring), lax.rem(me, ring)
+    rows = self_q.shape[1]
+    query_total = count * rows
+    context_rows = text_kv.shape[2]
+    key_total = ring * context_rows
+    self_span = own_q.shape[2]
+    text_span = text_rows.shape[2]
+    self_heads, text_heads = self_span // HEAD_DIM, text_span // HEAD_DIM
+
+    def peer(step):
+        return lax.rem(me + step, count)
+
+    def near(step):
+        return half * ring + lax.rem(place + step, ring)
+
+    def self_cols(device):
+        return pl.ds(pl.multiple_of(device * self_span, self_span), self_span)
+
+    def text_cols(device):
+        return pl.ds(pl.multiple_of(lax.rem(device, ring) * text_span, text_span), text_span)
+
+    def remote(kind, step, source, target, device):
+        return pltpu.make_async_remote_copy(
+            src_ref=source,
+            dst_ref=target,
+            send_sem=send_sem.at[kind, step],
+            recv_sem=recv_sem.at[kind, step],
+            device_id={"seq": device},
+            device_id_type=MESH,
+        )
+
+    kept = [
+        pltpu.make_async_copy(text_q.at[0, :, text_cols(me)], text_rows.at[me], local_sem.at[0]),
+        pltpu.make_async_copy(text_kv.at[0, :, :, text_cols(me)], context.at[place], local_sem.at[1]),
+        pltpu.make_async_copy(self_q.at[0, :, self_cols(me)], own_q.at[me], local_sem.at[2]),
+        pltpu.make_async_copy(self_k.at[0, :, self_cols(me)], own_k.at[me], local_sem.at[3]),
+        pltpu.make_async_copy(self_v.at[0, :, self_cols(me)], own_v.at[me], local_sem.at[4]),
+    ]
+    for copy in kept:
+        copy.start()
+
+    barrier = pltpu.get_barrier_semaphore()
+    for step in range(1, count):
+        pl.semaphore_signal(barrier, inc=1, device_id={"seq": peer(step)}, device_id_type=MESH)
+    pl.semaphore_wait(barrier, count - 1)
+
+    text_in, self_in = [], []
+    for step in range(1, count):
+        to = peer(step)
+        text_in.append(remote(0, step, text_q.at[0, :, text_cols(to)], text_rows.at[me], to))
+    for step in range(1, ring):
+        to = near(step)
+        text_in.append(remote(1, step, text_kv.at[0, :, :, text_cols(to)], context.at[place], to))
+    for kind, source, target in ((2, self_q, own_q), (3, self_k, own_k), (4, self_v, own_v)):
+        for step in range(1, count):
+            to = peer(step)
+            self_in.append(remote(kind, step, source.at[0, :, self_cols(to)], target.at[me], to))
+    for copy in text_in + self_in:
+        copy.start()
+
+    for copy in kept[:2]:
+        copy.wait()
+    for copy in text_in:
+        copy.wait_recv()
+    length = text_len[branch]
+    live = half * key_total + lax.broadcasted_iota(jnp.int32, (1, key_total), 1) < length
+    lane = lax.broadcasted_iota(jnp.int32, (query_total, HEAD_DIM), 1)
+    stats = jnp.full((query_total, HEAD_DIM), FAR, jnp.float32)
+    for head in range(text_heads):
+        span = slice(head * HEAD_DIM, (head + 1) * HEAD_DIM)
+        mixed, top, total = attend(
+            text_rows[:, :, span].reshape(query_total, HEAD_DIM),
+            context[:, 0, :, span].reshape(key_total, HEAD_DIM),
+            context[:, 1, :, span].reshape(key_total, HEAD_DIM),
+            live,
+        )
+        safe = jnp.where(total > 0.0, total, 1.0)
+        weight = jnp.where(total > 0.0, top + jnp.log(safe), FAR)
+        text_part[:, :, span] = (mixed / safe).astype(jnp.bfloat16).reshape(count, rows, HEAD_DIM)
+        stats = jnp.where(lane == head, weight, stats)
+    stat_part[...] = stats.reshape(count, rows, HEAD_DIM)
+    kept.append(pltpu.make_async_copy(text_part.at[me], text_back.at[half, :, text_cols(me)], local_sem.at[5]))
+    kept.append(pltpu.make_async_copy(stat_part.at[me], stat_back.at[me], local_sem.at[6]))
+    kept[5].start()
+    kept[6].start()
+    text_return = []
+    for step in range(1, count):
+        to = peer(step)
+        text_return.append(remote(6, step, stat_part.at[to], stat_back.at[me], to))
+        text_return.append(remote(5, step, text_part.at[to], text_back.at[half, :, text_cols(me)], to))
+    for copy in text_return:
+        copy.start()
+
+    for copy in kept[2:5]:
+        copy.wait()
+    for copy in self_in:
+        copy.wait_recv()
+    for head in range(self_heads):
+        span = slice(head * HEAD_DIM, (head + 1) * HEAD_DIM)
+        mixed, top, total = attend(
+            own_q[:, :, span].reshape(query_total, HEAD_DIM),
+            own_k[:, :, span].reshape(query_total, HEAD_DIM),
+            own_v[:, :, span].reshape(query_total, HEAD_DIM),
+            None,
+        )
+        self_part[:, :, span] = (mixed / total).astype(jnp.bfloat16).reshape(count, rows, HEAD_DIM)
+    kept.append(pltpu.make_async_copy(self_part.at[me], self_out.at[0, :, self_cols(me)], local_sem.at[7]))
+    kept[7].start()
+    self_return = []
+    for step in range(1, count):
+        to = peer(step)
+        self_return.append(remote(7, step, self_part.at[to], self_out.at[0, :, self_cols(me)], to))
+    for copy in self_return:
+        copy.start()
+
+    kept[5].wait()
+    kept[6].wait()
+    for copy in text_return:
+        copy.wait_recv()
+    for group in range(ring):
+        sides = [stat_back[side * ring + group] for side in range(HALVES)]
+        highest = functools.reduce(jnp.maximum, sides)
+        shares = [jnp.exp(side - highest) for side in sides]
+        whole = sum(shares)
+        shares = [share / whole for share in shares]
+        for head in range(text_heads):
+            start = group * text_span + head * HEAD_DIM
+            span = slice(start, start + HEAD_DIM)
+            merged = sum(
+                text_back[side, :, span].astype(jnp.float32) * shares[side][:, head : head + 1]
+                for side in range(HALVES)
+            )
+            text_out[0, :, span] = merged.astype(jnp.bfloat16)
+
+    kept[7].wait()
+    for copy in self_return:
+        copy.wait_recv()
+    for copy in text_in + self_in + text_return + self_return:
+        copy.wait_send()
+
+
+def fused_shards(self_queries, self_keys, self_values, text_queries, text_kv, text_len):
+    count = lax.axis_size("seq")
+    rows, channels = self_queries.shape[1:]
+    context_rows = text_kv.shape[2]
+    ring = count // HALVES
+    self_span, text_span = channels // count, channels // ring
+    in_place = pl.BlockSpec(memory_space=pl.ANY)
+    bf16, f32 = jnp.bfloat16, jnp.float32
+    out = jax.ShapeDtypeStruct((1, rows, channels), bf16)
+    return pl.pallas_call(
+        functools.partial(fused, count),
+        out_shape=(out, out),
+        in_specs=[in_place] * 5 + [pl.BlockSpec(memory_space=pltpu.SMEM)],
+        out_specs=(in_place, pl.BlockSpec(memory_space=pltpu.VMEM)),
+        scratch_shapes=[
+            pltpu.VMEM((count, rows, self_span), bf16),
+            pltpu.VMEM((count, rows, self_span), bf16),
+            pltpu.VMEM((count, rows, self_span), bf16),
+            pltpu.VMEM((count, rows, text_span), bf16),
+            pltpu.VMEM((ring, 2, context_rows, text_span), bf16),
+            pltpu.VMEM((count, rows, self_span), bf16),
+            pltpu.VMEM((count, rows, text_span), bf16),
+            pltpu.VMEM((count, rows, HEAD_DIM), f32),
+            pltpu.VMEM((HALVES, rows, channels), bf16),
+            pltpu.VMEM((count, rows, HEAD_DIM), f32),
+            pltpu.SemaphoreType.DMA((8, count)),
+            pltpu.SemaphoreType.DMA((8, count)),
+            pltpu.SemaphoreType.DMA((8,)),
+        ],
+        compiler_params=pltpu.CompilerParams(collective_id=0, has_side_effects=True),
+        name="attention",
+    )(self_queries, self_keys, self_values, text_queries, text_kv, text_len)
+
+
 def solution(mesh):
+    count = mesh.shape["seq"]
+    fits = count % HALVES == 0 and HEADS % count == 0
     return jax.shard_map(
-        shards,
+        fused_shards if fits else shards,
         mesh=mesh,
         in_specs=(
             P("enc", ("groups", "seq"), None),

time: 97.1 us -> 42.9 us (0.44)
  waiting for transfers between devices: 53.4 us -> 0 us
  Pallas kernels: 0 us -> 39.9 us
  starting transfers between devices: 27.9 us -> 0 us
  local copies, waits for them, and re-layouts: 11.7 us -> 2.26 us
  matrix products: 1.23 us -> 0 us
  other arithmetic: 1.08 us -> 0 us
    all_to_all x7 -> x0, waiting for transfers between devices: 53.4 us -> none  [the longest x1 17.8 us: shards(): lax.all_to_all(spread.reshape(1, 2, context_rows, seq_count, head_span),...]
    pallas_call x0 -> x1, Pallas kernels: none -> 39.9 us  [fused_shards(): pl.pallas_call(functools.partial(fused, count), out_shape=(out, out), in_...]
    all_to_all x7 -> x0, starting transfers between devices: 27.9 us -> none  [the longest x1 7.28 us: shards(): lax.all_to_all(head_view(text_queries), 'seq', split_axis=2, concat_axis=...]
    another operation x5 -> x0, local copies, waits for them, and re-layouts: 4.74 us -> none  [the longest x2 2.23 us: repeated(): return spread.reshape(1, token_rows, seq_count, head_span)]
    reshape x4 -> x0, local copies, waits for them, and re-layouts: 4.66 us -> none  [the longest x2 3.22 us: head_view(): return tensor.reshape(1, share_rows, seq_count, head_span)]
    unnamed x6 -> x4, local copies, waits for them, and re-layouts: 0.66 us -> 2.26 us
    dot_general x4 -> x0, matrix products: 1.23 us -> none  [the longest x2 0.63 us: absorb(): jnp.einsum('pqk,kpd->pqd', weights.astype(jnp.bfloat16), value_rows, pref...]
  transfers between devices with their start and end apart: 7 -> 0, of which waited for: 7 -> 0; matrix products, arithmetic and copies ran while one was open for 11% -> 0% of each run, Pallas kernels for 0% -> 0%
where the time goes in v1:
time: 42.9 us; the launch traced here: 42.8 us
  Pallas kernels  39.9 us (93%)
  local copies, waits for them, and re-layouts  2.26 us (5%)
  between operations  0.65 us (2%)
    pallas_call x1, Pallas kernels, fused_shards(): pl.pallas_call(functools.partial(fused, count), out_shape=(out, out), in_...  39.9 us
    unnamed x4, local copies, waits for them, and re-layouts  2.26 us

profile of v1, /device:TPU:0, one launch (start us, length us, event | category | flops | bytes accessed | tf_op | source)
XLA Modules:
  0.0 42.8 jit_solution(11329629382397678214)
XLA Ops:
  0.6 39.9 %attention.1 = (bf16[1,16,4096]{2,1,0:T(8,128)(2,1)}, bf16[1,16,4096]{2,1,0:T(8,128)(2,1)}) custom-call(bf16[1,16,4096]{2,1,0:T(8,128)(2,1)} %self_q.1, bf16[1,16,4096]{2,1,0:T(8,128)(2,1)} %self_k.1, bf16[1,16,4096]{2,1,0:T(8,128)(2,1)} %self_v.1, bf16[1,16,4096]{2,1,0:T(8,128)(2,1)} %text_q.1, bf16[1,2,64,4096]{3,2,1,0:T(8,128)(2,1)} %text_kv.1, s32[2]{0:T(128)} %text_len.1), custom_call_target="tpu_custom_call" | custom-call | tf_op jit(solution)/shard_map/attention/pallas_call | solution.py:337
  40.5 0.0 copy-start
  40.5 1.6 %copy.10 = bf16[1,16,4096]{2,1,0:T(8,128)(2,1)} copy(bf16[1,16,4096]{2,1,0:T(8,128)(2,1)} %get-tuple-element.4) | data formatting | bytes 262144
  42.1 0.0 copy-done
  42.1 0.7 %copy.11 = bf16[1,16,4096]{2,1,0:T(8,128)(2,1)} copy(bf16[1,16,4096]{2,1,0:T(8,128)(2,1)S(1)} %copy-done) | data formatting | bytes 262144
Async XLA Ops:
  40.5 1.6 %copy-start = (bf16[1,16,4096]{2,1,0:T(8,128)(2,1)S(1)}, bf16[1,16,4096]{2,1,0:T(8,128)(2,1)}, u32[]{:S(2)}) copy-start(bf16[1,16,4096]{2,1,0:T(8,128)(2,1)} %get-tuple-element.5) | copy-start | bytes 393220

commit v2 on v1

--- a/solution.py
+++ b/solution.py
@@ -177,6 +177,7 @@
     stat_part,
     text_back,
     stat_back,
+    stat_cols,
     send_sem,
     recv_sem,
     local_sem,
@@ -264,15 +265,15 @@
         weight = jnp.where(total > 0.0, top + jnp.log(safe), FAR)
         text_part[:, :, span] = (mixed / safe).astype(jnp.bfloat16).reshape(count, rows, HEAD_DIM)
         stats = jnp.where(lane == head, weight, stats)
-    stat_part[...] = stats.reshape(count, rows, HEAD_DIM)
+    stat_part[...] = stats.T[:text_heads]
     kept.append(pltpu.make_async_copy(text_part.at[me], text_back.at[half, :, text_cols(me)], local_sem.at[5]))
-    kept.append(pltpu.make_async_copy(stat_part.at[me], stat_back.at[me], local_sem.at[6]))
+    kept.append(pltpu.make_async_copy(stat_part, stat_back.at[me], local_sem.at[6]))
     kept[5].start()
     kept[6].start()
     text_return = []
     for step in range(1, count):
         to = peer(step)
-        text_return.append(remote(6, step, stat_part.at[to], stat_back.at[me], to))
+        text_return.append(remote(6, step, stat_part, stat_back.at[me], to))
         text_return.append(remote(5, step, text_part.at[to], text_back.at[half, :, text_cols(me)], to))
     for copy in text_return:
         copy.start()
@@ -303,26 +304,41 @@
     kept[6].wait()
     for copy in text_return:
         copy.wait_recv()
-    for group in range(ring):
-        sides = [stat_back[side * ring + group] for side in range(HALVES)]
-        highest = functools.reduce(jnp.maximum, sides)
-        shares = [jnp.exp(side - highest) for side in sides]
-        whole = sum(shares)
-        shares = [share / whole for share in shares]
-        for head in range(text_heads):
-            start = group * text_span + head * HEAD_DIM
-            span = slice(start, start + HEAD_DIM)
-            merged = sum(
-                text_back[side, :, span].astype(jnp.float32) * shares[side][:, head : head + 1]
-                for side in range(HALVES)
-            )
-            text_out[0, :, span] = merged.astype(jnp.bfloat16)
+    stat_cols[...] = stat_back[...].reshape(HALVES * HEADS, query_total).T
+    mine = stat_cols[pl.ds(pl.multiple_of(me * rows, rows), rows), :]
+    sides = [mine[:, side * HEADS : (side + 1) * HEADS] for side in range(HALVES)]
+    highest = functools.reduce(jnp.maximum, sides)
+    shares = [jnp.exp(side - highest) for side in sides]
+    whole = sum(shares)
+    shares = [share / whole for share in shares]
+    for head in range(HEADS):
+        span = slice(head * HEAD_DIM, (head + 1) * HEAD_DIM)
+        merged = sum(
+            text_back[side, :, span].astype(jnp.float32) * shares[side][:, head : head + 1]
+            for side in range(HALVES)
+        )
+        text_out[0, :, span] = merged.astype(jnp.bfloat16)
 
     kept[7].wait()
     for copy in self_return:
         copy.wait_recv()
     for copy in text_in + self_in + text_return + self_return:
         copy.wait_send()
+
+
+def carry(*refs):
+    sources, targets, held, sem = refs[0:2], refs[2:4], refs[4:6], refs[6]
+    steps = []
+    for n in range(2):
+        steps.append(pltpu.make_async_copy(sources[n], held[n], sem.at[0, n]))
+        steps[n].start()
+    ends = []
+    for n in range(2):
+        steps[n].wait()
+        ends.append(pltpu.make_async_copy(held[n], targets[n], sem.at[1, n]))
+        ends[n].start()
+    for end in ends:
+        end.wait()
 
 
 def fused_shards(self_queries, self_keys, self_values, text_queries, text_kv, text_len):
@@ -334,7 +350,7 @@
     in_place = pl.BlockSpec(memory_space=pl.ANY)
     bf16, f32 = jnp.bfloat16, jnp.float32
     out = jax.ShapeDtypeStruct((1, rows, channels), bf16)
-    return pl.pallas_call(
+    results = pl.pallas_call(
         functools.partial(fused, count),
         out_shape=(out, out),
         in_specs=[in_place] * 5 + [pl.BlockSpec(memory_space=pltpu.SMEM)],
@@ -347,9 +363,10 @@
             pltpu.VMEM((ring, 2, context_rows, text_span), bf16),
             pltpu.VMEM((count, rows, self_span), bf16),
             pltpu.VMEM((count, rows, text_span), bf16),
-            pltpu.VMEM((count, rows, HEAD_DIM), f32),
+            pltpu.VMEM((text_span // HEAD_DIM, count * rows), f32),
             pltpu.VMEM((HALVES, rows, channels), bf16),
-            pltpu.VMEM((count, rows, HEAD_DIM), f32),
+            pltpu.VMEM((count, text_span // HEAD_DIM, count * rows), f32),
+            pltpu.VMEM((count * rows, HALVES * HEADS), f32),
             pltpu.SemaphoreType.DMA((8, count)),
             pltpu.SemaphoreType.DMA((8, count)),
             pltpu.SemaphoreType.DMA((8,)),
@@ -357,6 +374,18 @@
         compiler_params=pltpu.CompilerParams(collective_id=0, has_side_effects=True),
         name="attention",
     )(self_queries, self_keys, self_values, text_queries, text_kv, text_len)
+    return pl.pallas_call(
+        carry,
+        out_shape=(out, out),
+        in_specs=[in_place] * 2,
+        out_specs=(in_place, in_place),
+        scratch_shapes=[
+            pltpu.VMEM((1, rows, channels), bf16),
+            pltpu.VMEM((1, rows, channels), bf16),
+            pltpu.SemaphoreType.DMA((2, 2)),
+        ],
+        name="carry",
+    )(*results)
 
 
 def solution(mesh):

time: 42.9 us -> 42.2 us (0.984)
  local copies, waits for them, and re-layouts: 2.26 us -> 0 us
  Pallas kernels: 39.9 us -> 41.4 us
    unnamed x4 -> x0, local copies, waits for them, and re-layouts: 2.26 us -> none
    pallas_call x0 -> x1, Pallas kernels: none -> 1.66 us  [fused_shards(): pl.pallas_call(carry, out_shape=(out, out), in_specs=[in_place] * 2, out_...]
where the time goes in v2:
time: 42.2 us; the launch traced here: 42.1 us
  Pallas kernels  41.4 us (98%)
  between operations  0.64 us (2%)
    pallas_call x1, Pallas kernels, fused_shards(): pl.pallas_call(functools.partial(fused, count), out_shape=(out, out), in_...  39.8 us
    pallas_call x1, Pallas kernels, fused_shards(): pl.pallas_call(carry, out_shape=(out, out), in_specs=[in_place] * 2, out_...  1.66 us

profile of v2, /device:TPU:0, one launch (start us, length us, event | category | flops | bytes accessed | tf_op | source)
XLA Modules:
  0.0 42.1 jit_solution(13048964293030565007)
XLA Ops:
  0.6 39.8 %attention.1 = (bf16[1,16,4096]{2,1,0:T(8,128)(2,1)}, bf16[1,16,4096]{2,1,0:T(8,128)(2,1)}) custom-call(bf16[1,16,4096]{2,1,0:T(8,128)(2,1)} %self_q.1, bf16[1,16,4096]{2,1,0:T(8,128)(2,1)} %self_k.1, bf16[1,16,4096]{2,1,0:T(8,128)(2,1)} %self_v.1, bf16[1,16,4096]{2,1,0:T(8,128)(2,1)} %text_q.1, bf16[1,2,64,4096]{3,2,1,0:T(8,128)(2,1)} %text_kv.1, s32[2]{0:T(128)} %text_len.1), custom_call_target="tpu_custom_call" | custom-call | tf_op jit(solution)/shard_map/attention/pallas_call | solution.py:353
  40.4 1.7 %carry.1 = (bf16[1,16,4096]{2,1,0:T(8,128)(2,1)}, bf16[1,16,4096]{2,1,0:T(8,128)(2,1)}) custom-call(bf16[1,16,4096]{2,1,0:T(8,128)(2,1)} %get-tuple-element.4.refs_0_, bf16[1,16,4096]{2,1,0:T(8,128)(2,1)} %get-tuple-element.5.refs_1_), custom_call_target="tpu_custom_call" | custom-call | tf_op jit(solution)/shard_map/carry/pallas_call | solution.py:377

commit v3 on v2

--- a/solution.py
+++ b/solution.py
@@ -242,7 +242,8 @@
         for step in range(1, count):
             to = peer(step)
             self_in.append(remote(kind, step, source.at[0, :, self_cols(to)], target.at[me], to))
-    for copy in text_in + self_in:
+    order = [kind * (count - 1) + step - 1 for step in range(1, count) for kind in range(3)]
+    for copy in text_in + [self_in[n] for n in order]:
         copy.start()
 
     for copy in kept[:2]:

time: 42.2 us -> 42.1 us (level)
  no operation moved by 1% of the time
where the time goes in v3:
time: 42.1 us; the launch traced here: 41.9 us
  Pallas kernels  41.3 us (98%)
  between operations  0.64 us (2%)
    pallas_call x1, Pallas kernels, fused_shards(): pl.pallas_call(functools.partial(fused, count), out_shape=(out, out), in_...  39.7 us
    pallas_call x1, Pallas kernels, fused_shards(): pl.pallas_call(carry, out_shape=(out, out), in_specs=[in_place] * 2, out_...  1.66 us

profile of v3, /device:TPU:0, one launch (start us, length us, event | category | flops | bytes accessed | tf_op | source)
XLA Modules:
  0.0 41.9 jit_solution(5161089833428148231)
XLA Ops:
  0.6 39.7 %attention.1 = (bf16[1,16,4096]{2,1,0:T(8,128)(2,1)}, bf16[1,16,4096]{2,1,0:T(8,128)(2,1)}) custom-call(bf16[1,16,4096]{2,1,0:T(8,128)(2,1)} %self_q.1, bf16[1,16,4096]{2,1,0:T(8,128)(2,1)} %self_k.1, bf16[1,16,4096]{2,1,0:T(8,128)(2,1)} %self_v.1, bf16[1,16,4096]{2,1,0:T(8,128)(2,1)} %text_q.1, bf16[1,2,64,4096]{3,2,1,0:T(8,128)(2,1)} %text_kv.1, s32[2]{0:T(128)} %text_len.1), custom_call_target="tpu_custom_call" | custom-call | tf_op jit(solution)/shard_map/attention/pallas_call | solution.py:354
  40.3 1.7 %carry.1 = (bf16[1,16,4096]{2,1,0:T(8,128)(2,1)}, bf16[1,16,4096]{2,1,0:T(8,128)(2,1)}) custom-call(bf16[1,16,4096]{2,1,0:T(8,128)(2,1)} %get-tuple-element.4.refs_0_, bf16[1,16,4096]{2,1,0:T(8,128)(2,1)} %get-tuple-element.5.refs_1_), custom_call_target="tpu_custom_call" | custom-call | tf_op jit(solution)/shard_map/carry/pallas_call | solution.py:378
